TPU v7x, 128 devices: a whole 4x4x4 slice. The times are simulated.
128 devices in a mesh: seg: 8 (over y_lo, z), grp: 16 (over x, y_hi, core).
Axes of the slice: x: 4, y: 4 (y_hi: 2, y_lo: 2; y = y_hi * 2 + y_lo), z: 4, core: 2. Of those that a mesh axis runs over, the one named last changes fastest.
Arguments:
- frames_in: bfloat16 [128, 32, 120, 128], P(('seg', 'grp')), may hold values from -6 to 6
- spatial_weight: bfloat16 [9, 128, 128], replicated, may hold values from -0.1875 to 0.1875
- temporal_weight: bfloat16 [2, 5, 128, 128], replicated, may hold values from -0.25 to 0.25
- uniting_weight: bfloat16 [2, 128, 128], replicated, may hold values from -0.375 to 0.375
- key_index: int32 [8], replicated, may hold values from 0 to 15
- dilation: int32 [2], replicated, may hold values from 1 to 8, as said below
- cotangent: bfloat16 [128, 32, 120, 128], P(('seg', 'grp')), may hold values from -6 to 6
Outputs:
- united: bfloat16 [128, 32, 120, 128], P(('seg', 'grp'))
- grad_frames: bfloat16 [128, 32, 120, 128], P(('seg', 'grp'))
- grad_spatial: float32 [9, 128, 128], replicated
- grad_temporal: float32 [2, 5, 128, 128], replicated
- grad_uniting: float32 [2, 128, 128], replicated
Inputs may be any that keep to these rules, and one draw needn't show every extreme that they name: `key_index`: position of a segment's keyframe within its 16 frames. Exactly one layer uses dilation 8; the others use less.
All inputs are finite; a program needn't handle non-finite values.
Results may differ from a plain program's by a relative error of at most 0.0095.
Values may be sent and summed in bfloat16 or wider, within the bound.
A program may use at most 128 MiB of HBM per device.

v0:
```python
import jax
import jax.numpy as jnp
from jax import lax
from jax.sharding import PartitionSpec as P

LAYERS = 2
DMAX = 8


def from_root(value, axis, root):
    mine = lax.axis_index(axis) == root
    return lax.psum(jnp.where(mine, value, jnp.zeros_like(value)), axis)


def silu_grad(value):
    sigma = jax.nn.sigmoid(value)
    return sigma * (1.0 + value * (1.0 - sigma))


def inner(left, right):
    return lax.dot_general(
        left, right, (((0,), (0,)), ((), ())), preferred_element_type=jnp.float32
    )


def spatial_forward(frames, kernel):
    count, rows, cols, chans = frames.shape
    padded = jnp.pad(frames, ((0, 0), (1, 1), (1, 1), (0, 0)))
    total = jnp.zeros((count * rows * cols, chans), jnp.float32)
    for row_tap in range(3):
        for col_tap in range(3):
            piece = padded[:, row_tap : row_tap + rows, col_tap : col_tap + cols, :].reshape(
                -1, chans
            )
            total = total + jnp.dot(
                piece, kernel[3 * row_tap + col_tap], preferred_element_type=jnp.float32
            )
    return total.reshape(frames.shape)


def spatial_back(grads, kernel):
    count, rows, cols, chans = grads.shape
    padded = jnp.pad(grads, ((0, 0), (1, 1), (1, 1), (0, 0)))
    total = jnp.zeros((count * rows * cols, chans), jnp.float32)
    for row_tap in range(3):
        for col_tap in range(3):
            piece = padded[
                :, 2 - row_tap : 2 - row_tap + rows, 2 - col_tap : 2 - col_tap + cols, :
            ].reshape(-1, chans)
            total = total + jnp.dot(
                piece, kernel[3 * row_tap + col_tap].T, preferred_element_type=jnp.float32
            )
    return total.reshape(grads.shape)


def spatial_wgrad(frames, grads):
    count, rows, cols, chans = frames.shape
    padded = jnp.pad(frames, ((0, 0), (1, 1), (1, 1), (0, 0)))
    flat_grads = grads.reshape(-1, chans)
    result = []
    for row_tap in range(3):
        for col_tap in range(3):
            piece = padded[:, row_tap : row_tap + rows, col_tap : col_tap + cols, :].reshape(
                -1, chans
            )
            result.append(inner(piece, flat_grads))
    return jnp.stack(result)


def shifted(values, offset):
    padded = jnp.pad(values, ((2 * DMAX, 2 * DMAX), (0, 0), (0, 0)))
    start = 2 * DMAX + offset
    return lax.dynamic_slice_in_dim(padded, start, values.shape[0], 0)


def temporal_forward(acts, kernel, step_size):
    chans = acts.shape[2]
    total = jnp.zeros((acts.shape[0] * acts.shape[1], chans), jnp.float32)
    for tap in range(5):
        piece = shifted(acts, (tap - 2) * step_size).reshape(-1, chans)
        total = total + jnp.dot(piece, kernel[tap], preferred_element_type=jnp.float32)
    return total.reshape(acts.shape)


def temporal_back(grads, kernel, step_size):
    chans = grads.shape[2]
    total = jnp.zeros((grads.shape[0] * grads.shape[1], chans), jnp.float32)
    for tap in range(5):
        piece = shifted(grads, (2 - tap) * step_size).reshape(-1, chans)
        total = total + jnp.dot(piece, kernel[tap].T, preferred_element_type=jnp.float32)
    return total.reshape(grads.shape)


def temporal_wgrad(acts, grads, step_size):
    chans = acts.shape[2]
    flat_grads = grads.reshape(-1, chans)
    return jnp.stack(
        [
            inner(shifted(acts, (tap - 2) * step_size).reshape(-1, chans), flat_grads)
            for tap in range(5)
        ]
    )


def to_pixels(flat):
    return lax.all_to_all(flat, ("seg", "grp"), split_axis=1, concat_axis=0, tiled=True)


def to_frames(blocks):
    return lax.all_to_all(blocks, ("seg", "grp"), split_axis=0, concat_axis=1, tiled=True)


def all_sum(parts):
    flat = jnp.concatenate([p.reshape(-1) for p in parts])
    count = lax.axis_size(("seg", "grp"))
    chunk = flat.shape[0] // count
    pieces = lax.all_to_all(
        flat.reshape(count, chunk), ("seg", "grp"), split_axis=0, concat_axis=0, tiled=True
    )
    mine = jnp.sum(pieces, axis=0)
    spread = jnp.broadcast_to(mine[None], (count, chunk))
    whole = lax.all_to_all(spread, ("seg", "grp"), split_axis=0, concat_axis=0, tiled=True)
    whole = whole.reshape(-1)
    out = []
    offset = 0
    for p in parts:
        out.append(whole[offset : offset + p.size].reshape(p.shape))
        offset += p.size
    return out


def local(
    frames_in, spatial_weight, temporal_weight, uniting_weight, key_index, dilation, cotangent
):
    local_frames, rows, cols, chans = frames_in.shape
    pixels = rows * cols
    seg_count = lax.axis_size("seg")
    pre_spatial = spatial_forward(frames_in, spatial_weight)
    act_zero = jax.nn.silu(pre_spatial).astype(jnp.bfloat16).reshape(local_frames, pixels, chans)
    cot_local = cotangent.reshape(local_frames, pixels, chans)
    act_blocks = to_pixels(act_zero)
    cot_blocks = to_pixels(cot_local)
    acts = [act_blocks]
    total_frames = acts[0].shape[0]
    block = acts[0].shape[1]
    seg_frames = total_frames // seg_count
    pres = []
    for layer in range(LAYERS):
        pre = temporal_forward(acts[-1], temporal_weight[layer], dilation[layer])
        pres.append(pre)
        acts.append(jax.nn.silu(pre).astype(jnp.bfloat16))
    feat = acts[-1]
    feat_seg = feat.reshape(seg_count, seg_frames, block, chans)
    positions = jnp.arange(seg_frames, dtype=jnp.int32)
    onehot = positions[None, :] == key_index[:, None]
    keys = jnp.einsum(
        "ns,nspc->npc", onehot.astype(jnp.bfloat16), feat_seg, preferred_element_type=jnp.float32
    ).astype(jnp.bfloat16)
    key_full = jnp.broadcast_to(keys[:, None], feat_seg.shape).reshape(-1, chans)
    feat_flat = feat.reshape(-1, chans)
    key_part = jnp.dot(
        keys.reshape(-1, chans), uniting_weight[1], preferred_element_type=jnp.float32
    ).reshape(seg_count, 1, block, chans)
    main_part = jnp.dot(feat_flat, uniting_weight[0], preferred_element_type=jnp.float32)
    united_blocks = (
        (main_part.reshape(seg_count, seg_frames, block, chans) + key_part)
        .astype(jnp.bfloat16)
        .reshape(total_frames, block, chans)
    )
    united = to_frames(united_blocks)
    cot_flat = cot_blocks.reshape(-1, chans)
    grad_feat = jnp.dot(cot_flat, uniting_weight[0].T, preferred_element_type=jnp.float32)
    seg_cot = jnp.sum(
        cot_blocks.reshape(seg_count, seg_frames, block, chans).astype(jnp.float32), axis=1
    )
    key_term = jnp.dot(
        seg_cot.reshape(-1, chans),
        uniting_weight[1].T.astype(jnp.float32),
        precision=lax.Precision.HIGHEST,
    ).reshape(seg_count, 1, block, chans)
    placed = onehot.astype(jnp.float32)[:, :, None, None] * key_term
    grad_feat = grad_feat.reshape(seg_count, seg_frames, block, chans) + placed
    grad_feat = grad_feat.reshape(total_frames, block, chans)
    grad_uniting = jnp.stack([inner(feat_flat, cot_flat), inner(key_full, cot_flat)])
    grad_pre = (grad_feat * silu_grad(pres[-1])).astype(jnp.bfloat16)
    tgrads = [None] * LAYERS
    grad_act0 = None
    for layer in range(LAYERS - 1, -1, -1):
        tgrads[layer] = temporal_wgrad(acts[layer], grad_pre, dilation[layer])
        grad_act = temporal_back(grad_pre, temporal_weight[layer], dilation[layer])
        if layer > 0:
            grad_pre = (grad_act * silu_grad(pres[layer - 1])).astype(jnp.bfloat16)
        else:
            grad_act0 = grad_act.astype(jnp.bfloat16)
    grad_time = to_frames(grad_act0).reshape(frames_in.shape)
    grad_spre = (grad_time.astype(jnp.float32) * silu_grad(pre_spatial)).astype(jnp.bfloat16)
    grad_frames = spatial_back(grad_spre, spatial_weight).astype(jnp.bfloat16)
    grad_spatial = spatial_wgrad(frames_in, grad_spre)
    summed = all_sum((grad_spatial, jnp.stack(tgrads), grad_uniting))
    scale = 1.0 / jnp.sqrt(jnp.float32(total_frames * pixels))
    return (
        united.reshape(frames_in.shape),
        grad_frames,
        summed[0] * scale,
        summed[1] * scale,
        summed[2] * scale,
    )


def solution(mesh):
    placed = (
        P(("seg", "grp"), None, None, None),
        P(),
        P(),
        P(),
        P(),
        P(),
        P(("seg", "grp"), None, None, None),
    )
    return jax.shard_map(
        local,
        mesh=mesh,
        in_specs=placed,
        out_specs=(
            P(("seg", "grp"), None, None, None),
            P(("seg", "grp"), None, None, None),
            P(),
            P(),
            P(),
        ),
        check_vma=False,
    )
```

profile of v0, /device:TPU:1, one launch (start us, length us, event | category | flops | bytes accessed | tf_op | source)
XLA Modules:
  0.0 491.9 jit_solution(17420087802253160140)
XLA Ops:
  0.6 7.3 %pad_slice_fusion.8 = (bf16[1,32,120,128]{3,2,1,0:T(8,128)(2,1)S(1)}, bf16[1,32,120,128]{3,2,1,0:T(8,128)(2,1)S(1)}, bf16[1,32,120,128]{3,2,1,0:T(8,128)(2,1)S(1...) fusion(bf16[1,32,120,128]{3,2,1,0:T(8,128)(2,1)} %param.7), kind=kLoop, calls=%fused_computation.142 | loop fusion | bytes 8847360 | tf_op jit(solution)/shard_map/slice | solution.py:32
  12.9 16.0 %copy.296 = bf16[1,3840,128]{2,0,1:T(2,128)(2,1)} copy(bf16[1,3840,128]{2,1,0:T(8,128)(2,1)S(1)} %fusion.40) | data formatting | bytes 1966080 | tf_op jit(solution)/shard_map/convert_element_type | solution.py:139
  29.5 23.1 %reduce.5 = bf16[3840,128]{1,0:T(8,128)(2,1)} reduce(bf16[3840,1,128]{2,1,0:T(2,128)(2,1)} %bitcast.395, bf16[]{:T(256)} %broadcast.150), dimensions={1}, to_apply=%bitcast.387.reduce_sub_computation | reduce | bytes 1966082
  52.6 3.0 reshape.597
  55.6 12.3 %all-to-all-start = ((bf16[128,2,1920]{2,1,0:T(2,128)(2,1)}), bf16[128,2,1920]{2,1,0:T(2,128)(2,1)}, u32[]{:S(2)}, u32[]{:S(2)}) async-start(bf16[128,2,1920]{2,1,0:T(2,128)(2,1)} %reshape.597), calls=%async_computation | async-start | bytes 1966080 | tf_op jit(solution)/shard_map/all_to_all | solution.py:106
  76.5 9.9 %copy.295 = bf16[1,3840,128]{2,0,1:T(2,128)(2,1)} copy(bf16[1,3840,128]{2,1,0:T(8,128)(2,1)} %bitcast.418) | data formatting | bytes 1966080 | tf_op jit(solution)/shard_map/reshape | solution.py:140
  86.4 23.1 %reduce.6 = bf16[3840,128]{1,0:T(8,128)(2,1)} reduce(bf16[3840,1,128]{2,1,0:T(2,128)(2,1)} %bitcast.396, bf16[]{:T(256)} %broadcast.150), dimensions={1}, to_apply=%bitcast.386.reduce_sub_computation | reduce | bytes 1966082
  109.5 3.0 reshape.599
  114.4 10.7 %all-to-all-start.2 = ((bf16[128,2,1920]{2,1,0:T(2,128)(2,1)}), bf16[128,2,1920]{2,1,0:T(2,128)(2,1)}, u32[]{:S(2)}, u32[]{:S(2)}) async-start(bf16[128,2,1920]{2,1,0:T(2,128)(2,1)} %reshape.599), calls=%async_computation.2 | async-start | bytes 1966080 | tf_op jit(solution)/shard_map/all_to_all | solution.py:106
  125.2 4.1 reshape.598
  129.4 17.4 %bitcast_reduce_fusion.1 = bf16[3840,128]{1,0:T(8,128)(2,1)} fusion(bf16[3840,1,128]{2,1,0:T(2,128)(2,1)S(1)} %reshape.598), kind=kLoop, calls=%fused_computation.260 | loop fusion | bytes 1966080 | tf_op jit(solution)/shard_map/all_to_all | solution.py:106
  151.5 5.9 %pad_dynamic-slice_fusion.12 = (bf16[128,30,128]{0,2,1:T(8,128)(2,1)}, bf16[128,30,128]{0,2,1:T(8,128)(2,1)}, bf16[128,30,128]{0,2,1:T(8,128)(2,1)}, bf16[128,30,128]{0,2,1:T(8,128)(2,1)}) fusion(s32[]{:T(128)S(6)} %select_n.19, bf16[128,30,128]{0,2,1:T(8,128)(2,1)} %copy.205, s32[]{:T(128)S(6)} %select_n.17, s32[]{:T(128)S(6)} %select_n.18, s32[]{:T(128)S(6)} %select_n.16), kind=kLoop, calls=%fused_computation.46 | loop fusion | bytes 4915216 | tf_op jit(solution)/shard_map/dynamic_slice | solution.py:73
  157.4 2.6 copy.209
  162.2 2.6 copy.207
  167.1 2.6 copy.208
  171.9 2.6 copy.206
  182.3 2.7 multiply_convert_fusion.10
  186.2 2.7 reshape.525
  191.8 3.5 pad_dynamic-slice_fusion.8
  195.3 2.7 copy.215
  222.8 5.7 %reshape.600 = bf16[3840,1,128]{2,1,0:T(2,128)(2,1)} reshape(bf16[128,2,1920]{2,1,0:T(2,128)(2,1)} %all-to-all-done.2) | data formatting | bytes 1966080
  228.5 18.6 %bitcast_reduce_fusion = bf16[3840,128]{1,0:T(8,128)(2,1)} fusion(bf16[3840,1,128]{2,1,0:T(2,128)(2,1)} %reshape.600), kind=kLoop, calls=%fused_computation.259 | loop fusion | bytes 1966080 | tf_op jit(solution)/shard_map/all_to_all | solution.py:106
  250.9 5.0 %multiply_convert_fusion = (bf16[8,16,30,128]{3,2,1,0:T(8,128)(2,1)}, bf16[8,16,30,128]{3,2,1,0:T(8,128)(2,1)}, f32[8,16,30,128]{3,2,1,0:T(8,128)}) fusion(f32[8,16,30,128]{3,2,1,0:T(8,128)} %reshape.530, f32[8,30,128]{2,1,0:T(8,128)S(1)} %fusion.47, f32[8,16]{1,0:T(8,128)S(1)} %get-tuple-element.39, bf16[8,16,30,128]{3,2,1,0:T(8,128)(2,1)} %dot_general.221, ...), kind=kOutput, calls=%fused_computation.50 | convolution fusion | flops 132218880 | bytes 7049216 | tf_op jit(solution)/shard_map/dot_general | solution.py:172
  258.5 2.9 copy.219
  263.3 3.0 multiply_convert_fusion.8
  267.3 3.2 pad_dynamic-slice_fusion.4
  270.5 2.7 copy.223
  275.4 2.7 copy.221
  284.1 2.7 copy.220
  296.2 3.2 multiply_convert_fusion.5
  299.4 2.7 reshape.541
  302.1 2.9 copy.225
  305.0 3.0 multiply_convert_fusion.6
  309.1 3.5 pad_dynamic-slice_fusion
  314.8 3.0 convolution_bitcast_fusion.1
  321.6 3.1 convolution_bitcast_fusion
  355.3 10.2 %all-to-all-start.3 = ((bf16[128,30,128]{2,1,0:T(8,128)(2,1)}), bf16[128,30,128]{2,1,0:T(8,128)(2,1)}, u32[]{:S(2)}, u32[]{:S(2)}) async-start(bf16[128,30,128]{2,1,0:T(8,128)(2,1)} %convert_element_type.195), calls=%async_computation.3 | async-start | bytes 2097152 | tf_op jit(solution)/shard_map/all_to_all | solution.py:110
  371.1 13.0 %all-to-all-done.3 = bf16[128,30,128]{2,1,0:T(8,128)(2,1)} async-done(((bf16[128,30,128]{2,1,0:T(8,128)(2,1)}), bf16[128,30,128]{2,1,0:T(8,128)(2,1)}, u32[]{:S(2)}, u32[]{:S(2)}) %all-to-all-start.3) | async-done | bytes 983072 | tf_op jit(solution)/shard_map/all_to_all | solution.py:110
  384.1 5.2 %all-to-all-start.1 = ((bf16[128,30,128]{2,1,0:T(8,128)(2,1)}), bf16[128,30,128]{2,1,0:T(8,128)(2,1)}, u32[]{:S(2)}, u32[]{:S(2)}) async-start(bf16[128,30,128]{2,1,0:T(8,128)(2,1)} %bitcast.52), calls=%async_computation.1 | async-start | bytes 2097152 | tf_op jit(solution)/shard_map/all_to_all | solution.py:110
  389.4 2.6 copy.230
  394.0 4.2 multiply_convert_fusion.2
  398.3 2.7 copy.235
  420.4 3.6 pad_slice_fusion
  425.7 10.6 %all-to-all-start.4 = ((f32[128,1,2688]{2,1,0:T(1,128)}), f32[128,1,2688]{2,1,0:T(1,128)}, u32[]{:S(2)}, u32[]{:S(2)}) async-start(f32[128,1,2688]{2,1,0:T(1,128)} %bitcast.397), calls=%async_computation.4 | async-start | bytes 2752512 | tf_op jit(solution)/shard_map/all_to_all | solution.py:117
  436.4 3.6 convolution_add_fusion.7
  450.8 7.6 %all-to-all-done.4 = f32[128,1,2688]{2,1,0:T(1,128)} async-done(((f32[128,1,2688]{2,1,0:T(1,128)}), f32[128,1,2688]{2,1,0:T(1,128)}, u32[]{:S(2)}, u32[]{:S(2)}) %all-to-all-start.4) | async-done | bytes 1376288 | tf_op jit(solution)/shard_map/all_to_all | solution.py:117
  462.4 4.3 all-to-all-start.5
  473.4 15.9 %all-to-all-done.5 = f32[128,1,2688]{2,1,0:T(1,128)S(1)} async-done(((f32[128,1,2688]{2,1,0:T(1,128)}), f32[128,1,2688]{2,1,0:T(1,128)S(1)}, u32[]{:S(2)}, u32[]{:S(2)}) %all-to-all-start.5) | async-done | bytes 1376288 | tf_op jit(solution)/shard_map/all_to_all | solution.py:122
  (229 shorter events, 174.2 us)
Async XLA Ops:
  0.6 7.3 %copy-start.40 = (bf16[9,128,128]{2,1,0:T(8,128)(2,1)S(1)}, bf16[9,128,128]{2,1,0:T(8,128)(2,1)}, u32[]{:S(2)}) copy-start(bf16[9,128,128]{2,1,0:T(8,128)(2,1)} %param.8) | copy-start | bytes 884740
  12.4 62.6 %copy-start = (f32[3840,128]{1,0:T(8,128)}, f32[3840,128]{1,0:T(8,128)S(1)}, u32[]{:S(2)}) copy-start(f32[3840,128]{1,0:T(8,128)S(1)} %convolution_add_fusion.24) | copy-start | bytes 5898244
  52.6 15.3 %copy-start.51 = (s32[2]{0:T(128)S(1)}, s32[2]{0:T(128)}, u32[]{:S(2)}) copy-start(s32[2]{0:T(128)} %param.12) | copy-start | bytes 28
  55.6 58.8 %all-to-all-start = ((bf16[128,2,1920]{2,1,0:T(2,128)(2,1)}), bf16[128,2,1920]{2,1,0:T(2,128)(2,1)}, u32[]{:S(2)}, u32[]{:S(2)}) async-start(bf16[128,2,1920]{2,1,0:T(2,128)(2,1)} %reshape.597), calls=%async_computation | async-start | bytes 1966080 | tf_op jit(solution)/shard_map/all_to_all | solution.py:106
  86.4 26.1 %copy-start.18 = (f32[128,30,128]{2,1,0:T(8,128)S(1)}, f32[128,30,128]{2,1,0:T(8,128)}, u32[]{:S(2)}) copy-start(f32[128,30,128]{2,1,0:T(8,128)} %reshape.556) | copy-start | bytes 5898244
  112.5 1.9 copy-start.52
  114.4 108.4 %all-to-all-start.2 = ((bf16[128,2,1920]{2,1,0:T(2,128)(2,1)}), bf16[128,2,1920]{2,1,0:T(2,128)(2,1)}, u32[]{:S(2)}, u32[]{:S(2)}) async-start(bf16[128,2,1920]{2,1,0:T(2,128)(2,1)} %reshape.599), calls=%async_computation.2 | async-start | bytes 1966080 | tf_op jit(solution)/shard_map/all_to_all | solution.py:106
  129.4 50.3 %copy-start.4 = (bf16[3840,1,128]{2,1,0:T(2,128)(2,1)}, bf16[3840,1,128]{2,1,0:T(2,128)(2,1)S(1)}, u32[]{:S(2)}) copy-start(bf16[3840,1,128]{2,1,0:T(2,128)(2,1)S(1)} %reshape.598) | copy-start | bytes 2949124
  176.8 1.7 copy-start.31
  191.2 4.1 copy-start.3
  195.3 4.9 copy-start.14
  200.2 4.2 copy-start.12
  204.3 3.4 copy-start.16
  247.1 3.6 copy-start.49
  263.3 3.0 copy-start.17
  288.9 1.7 copy-start.29
  290.6 1.6 copy-start.20
  290.7 2.1 copy-start.38
  294.4 1.6 copy-start.37
  294.4 1.8 copy-start.44
  305.0 3.0 copy-start.10
  314.8 3.0 copy-start.47
  321.6 3.1 copy-start.15
  321.6 4.1 copy-start.41
  321.6 4.1 copy-start.53
  324.7 2.5 copy-start.13
  325.7 2.5 copy-start.11
  327.1 2.1 copy-start.9
  328.2 2.1 copy-start.5
  328.2 2.1 copy-start.42
  329.3 2.1 copy-start.8
  345.3 1.7 copy-start.30
  353.0 13.5 %copy-start.7 = (bf16[128,30,128]{0,2,1:T(8,128)(2,1)S(1)}, bf16[128,30,128]{0,2,1:T(8,128)(2,1)}, u32[]{:S(2)}) copy-start(bf16[128,30,128]{0,2,1:T(8,128)(2,1)} %get-tuple-element.27) | copy-start | bytes 2949124
  355.3 28.8 %all-to-all-start.3 = ((bf16[128,30,128]{2,1,0:T(8,128)(2,1)}), bf16[128,30,128]{2,1,0:T(8,128)(2,1)}, u32[]{:S(2)}, u32[]{:S(2)}) async-start(bf16[128,30,128]{2,1,0:T(8,128)(2,1)} %convert_element_type.195), calls=%async_computation.3 | async-start | bytes 2097152 | tf_op jit(solution)/shard_map/all_to_all | solution.py:110
  365.5 2.1 copy-start.48
  365.5 3.9 copy-start.50
  365.5 4.1 copy-start.21
  384.1 41.6 %all-to-all-start.1 = ((bf16[128,30,128]{2,1,0:T(8,128)(2,1)}), bf16[128,30,128]{2,1,0:T(8,128)(2,1)}, u32[]{:S(2)}, u32[]{:S(2)}) async-start(bf16[128,30,128]{2,1,0:T(8,128)(2,1)} %bitcast.52), calls=%async_computation.1 | async-start | bytes 2097152 | tf_op jit(solution)/shard_map/all_to_all | solution.py:110
  394.0 20.2 %copy-start.2 = (f32[128,30,128]{2,1,0:T(8,128)}, f32[128,30,128]{2,1,0:T(8,128)S(1)}, u32[]{:S(2)}) copy-start(f32[128,30,128]{2,1,0:T(8,128)S(1)} %copy.231) | copy-start | bytes 5898244
  403.1 2.4 copy-start.33
  414.2 1.5 copy-start.36
  415.7 2.4 copy-start.1
  425.7 32.7 %all-to-all-start.4 = ((f32[128,1,2688]{2,1,0:T(1,128)}), f32[128,1,2688]{2,1,0:T(1,128)}, u32[]{:S(2)}, u32[]{:S(2)}) async-start(f32[128,1,2688]{2,1,0:T(1,128)} %bitcast.397), calls=%async_computation.4 | async-start | bytes 2752512 | tf_op jit(solution)/shard_map/all_to_all | solution.py:117
  444.7 2.4 copy-start.26
  447.1 1.5 copy-start.39
  460.6 6.1 %copy-start.23 = (bf16[1,32,120,128]{3,2,1,0:T(8,128)(2,1)S(1)}, bf16[1,32,120,128]{3,2,1,0:T(8,128)(2,1)}, u32[]{:S(2)}) copy-start(bf16[1,32,120,128]{3,2,1,0:T(8,128)(2,1)} %get-tuple-element.11) | copy-start | bytes 2949124
  462.4 26.8 %all-to-all-start.5 = ((f32[128,1,2688]{2,1,0:T(1,128)}), f32[128,1,2688]{2,1,0:T(1,128)S(1)}, u32[]{:S(2)}, u32[]{:S(2)}) async-start(f32[128,1,2688]{2,1,0:T(1,128)} %broadcast_in_dim.5), calls=%async_computation.5 | async-start | bytes 2752512 | tf_op jit(solution)/shard_map/all_to_all | solution.py:122
  466.7 2.1 copy-start.22
  (12 other events, 15.2 us)
where the time goes:
time: 502 us; the launch traced here: 492 us
  local copies, waits for them, and re-layouts  235 us (47%)
  matrix products  87.9 us (18%)
  other arithmetic  70.9 us (14%)
  starting transfers between devices  53.4 us (11%)
  waiting for transfers between devices  36.5 us (7%)
  between operations  8.25 us (2%)
    dynamic_slice x20, local copies, waits for them, and re-layouts, shifted(): return lax.dynamic_slice_in_dim(padded, start, values.shape[0], 0)  53.4 us
    unnamed x2, other arithmetic  46.2 us
    all_to_all x4, local copies, waits for them, and re-layouts, to_pixels(): lax.all_to_all(flat, ('seg', 'grp'), split_axis=1, concat_axis=0, tiled=T...  40.8 us
    dot_general x21, matrix products, inner(): lax.dot_general(left, right, (((0,), (0,)), ((), ())), preferred_element_...  28.1 us
    all_to_all x2, starting transfers between devices, to_pixels(): lax.all_to_all(flat, ('seg', 'grp'), split_axis=1, concat_axis=0, tiled=T...  23 us
    unnamed x113, local copies, waits for them, and re-layouts  21.1 us
    dot_general x9, matrix products, spatial_back(): jnp.dot(piece, kernel[3 * row_tap + col_tap].T, preferred_element_type=jn...  17 us
    dot_general x10, matrix products, temporal_back(): jnp.dot(piece, kernel[tap].T, preferred_element_type=jnp.float32)  16.8 us
  transfers between devices with their start and end apart: 6, of which 3 were waited for; matrix products, arithmetic and copies ran while one was open for 40% of the time, Pallas kernels for 0%

commit v1 on v0

--- a/solution.py
+++ b/solution.py
@@ -107,7 +107,15 @@
 
 
 def to_frames(blocks):
-    return lax.all_to_all(blocks, ("seg", "grp"), split_axis=0, concat_axis=1, tiled=True)
+    return jnp.concatenate(
+        lax.all_to_all(
+            jnp.stack(jnp.split(blocks, lax.axis_size(("seg", "grp")), axis=0)),
+            ("seg", "grp"),
+            0,
+            0,
+        ),
+        axis=1,
+    )
 
 
 def all_sum(parts):

time: 502 us -> 615 us (1.23)
  local copies, waits for them, and re-layouts: 235 us -> 371 us
  matrix products: 87.9 us -> 71.7 us
    unnamed x113 -> x379, local copies, waits for them, and re-layouts: 21.1 us -> 176 us
    dot_general x21, matrix products: 28.1 us -> 16.1 us  [inner(): lax.dot_general(left, right, (((0,), (0,)), ((), ())), preferred_element_...]
  transfers between devices with their start and end apart: 6 -> 6, of which waited for: 3 -> 3; matrix products, arithmetic and copies ran while one was open for 40% -> 29% of each run, Pallas kernels for 0% -> 0%
where the time goes in v1:
time: 615 us; the launch traced here: 606 us
  local copies, waits for them, and re-layouts  371 us (60%)
  matrix products  71.7 us (12%)
  other arithmetic  66.1 us (11%)
  starting transfers between devices  52.4 us (9%)
  waiting for transfers between devices  35.9 us (6%)
  between operations  8.81 us (1%)
    unnamed x379, local copies, waits for them, and re-layouts  176 us
    dynamic_slice x20, local copies, waits for them, and re-layouts, shifted(): return lax.dynamic_slice_in_dim(padded, start, values.shape[0], 0)  49.4 us
    unnamed x2, other arithmetic  44.3 us
    all_to_all x4, local copies, waits for them, and re-layouts, to_pixels(): lax.all_to_all(flat, ('seg', 'grp'), split_axis=1, concat_axis=0, tiled=T...  37.9 us
    all_to_all x2, starting transfers between devices, to_pixels(): lax.all_to_all(flat, ('seg', 'grp'), split_axis=1, concat_axis=0, tiled=T...  22.7 us
    all_to_all x1, waiting for transfers between devices, all_sum(): lax.all_to_all(spread, ('seg', 'grp'), split_axis=0, concat_axis=0, tiled...  16.7 us
    reshape x8, local copies, waits for them, and re-layouts, temporal_forward(): piece = shifted(acts, (tap - 2) * step_size).reshape(-1, chans)  16.7 us
    dot_general x21, matrix products, inner(): lax.dot_general(left, right, (((0,), (0,)), ((), ())), preferred_element_...  16.1 us
  transfers between devices with their start and end apart: 6, of which 3 were waited for; matrix products, arithmetic and copies ran while one was open for 29% of the time, Pallas kernels for 0%

profile of v1, /device:TPU:1, one launch (start us, length us, event | category | flops | bytes accessed | tf_op | source)
XLA Modules:
  0.0 605.6 jit_solution(16425901323556292564)
XLA Ops:
  0.6 7.3 %pad_slice_fusion.8 = (bf16[1,32,120,128]{3,2,1,0:T(8,128)(2,1)S(1)}, bf16[1,32,120,128]{3,2,1,0:T(8,128)(2,1)S(1)}, bf16[1,32,120,128]{3,2,1,0:T(8,128)(2,1)S(1...) fusion(bf16[1,32,120,128]{3,2,1,0:T(8,128)(2,1)} %param.7), kind=kLoop, calls=%fused_computation.150 | loop fusion | bytes 8847360 | tf_op jit(solution)/shard_map/slice | solution.py:32
  12.9 16.0 %copy.618 = bf16[1,3840,128]{2,0,1:T(2,128)(2,1)} copy(bf16[1,3840,128]{2,1,0:T(8,128)(2,1)S(1)} %fusion.47) | data formatting | bytes 1966080 | tf_op jit(solution)/shard_map/convert_element_type | solution.py:147
  29.5 22.3 %reduce.5 = bf16[3840,128]{1,0:T(8,128)(2,1)S(1)} reduce(bf16[3840,1,128]{2,1,0:T(2,128)(2,1)} %bitcast.1440, bf16[]{:T(256)} %broadcast.166), dimensions={1}, to_apply=%bitcast.1432.reduce_sub_computation | reduce | bytes 1966082
  53.1 11.9 %all-to-all-start = ((bf16[128,2,1920]{2,1,0:T(2,128)(2,1)}), bf16[128,2,1920]{2,1,0:T(2,128)(2,1)S(1)}, u32[]{:S(2)}, u32[]{:S(2)}) async-start(bf16[128,2,1920]{2,1,0:T(2,128)(2,1)} %reshape.863), calls=%async_computation | async-start | bytes 1966080 | tf_op jit(solution)/shard_map/all_to_all | solution.py:106
  73.5 9.1 %copy.617 = bf16[1,3840,128]{2,0,1:T(2,128)(2,1)S(1)} copy(bf16[1,3840,128]{2,1,0:T(8,128)(2,1)} %bitcast.1592) | data formatting | bytes 1966080 | tf_op jit(solution)/shard_map/reshape | solution.py:148
  82.6 22.0 %reduce.6 = bf16[3840,128]{1,0:T(8,128)(2,1)} reduce(bf16[3840,1,128]{2,1,0:T(2,128)(2,1)S(1)} %bitcast.1441, bf16[]{:T(256)} %broadcast.166), dimensions={1}, to_apply=%bitcast.1431.reduce_sub_computation | reduce | bytes 1966082
  104.6 3.0 reshape.865
  108.7 10.8 %all-to-all-start.2 = ((bf16[128,2,1920]{2,1,0:T(2,128)(2,1)}), bf16[128,2,1920]{2,1,0:T(2,128)(2,1)}, u32[]{:S(2)}, u32[]{:S(2)}) async-start(bf16[128,2,1920]{2,1,0:T(2,128)(2,1)} %reshape.865), calls=%async_computation.2 | async-start | bytes 1966080 | tf_op jit(solution)/shard_map/all_to_all | solution.py:106
  119.5 4.1 reshape.864
  123.7 16.4 %bitcast_reduce_fusion.1 = bf16[3840,128]{1,0:T(8,128)(2,1)S(1)} fusion(bf16[3840,1,128]{2,1,0:T(2,128)(2,1)S(1)} %reshape.864), kind=kLoop, calls=%fused_computation.780 | loop fusion | bytes 1966080 | tf_op jit(solution)/shard_map/all_to_all | solution.py:106
  141.3 2.6 copy.530
  144.0 5.5 pad_dynamic-slice_fusion.12
  153.7 2.7 copy.532
  158.6 2.7 copy.533
  163.4 2.7 copy.531
  173.8 2.6 multiply_convert_fusion.9
  177.7 2.7 reshape.792
  183.2 3.5 pad_dynamic-slice_fusion.8
  186.8 2.8 copy.540
  208.5 3.0 multiply_convert_fusion.8
  211.5 2.7 reshape.797
  214.1 2.7 reshape.801
  216.8 5.6 reshape.866
  222.5 17.6 %bitcast_reduce_fusion = bf16[3840,128]{1,0:T(8,128)(2,1)S(1)} fusion(bf16[3840,1,128]{2,1,0:T(2,128)(2,1)} %reshape.866), kind=kLoop, calls=%fused_computation.779 | loop fusion | bytes 1966080 | tf_op jit(solution)/shard_map/all_to_all | solution.py:106
  243.0 5.0 multiply_convert_fusion
  248.0 2.6 reshape.804
  250.6 3.0 copy.544
  253.6 2.9 copy.542
  256.5 2.9 multiply_convert_fusion.7
  260.4 3.5 pad_dynamic-slice_fusion.4
  270.3 2.3 copy.547
  284.4 3.2 multiply_convert_fusion.4
  287.6 2.7 reshape.807
  290.3 2.9 copy.550
  293.2 3.0 multiply_convert_fusion.5
  297.2 3.4 pad_dynamic-slice_fusion
  302.8 3.0 convolution_bitcast_fusion.1
  309.9 3.0 convolution_bitcast_fusion
  485.7 9.8 %all-to-all-start.3 = ((bf16[128,1,30,128]{3,2,1,0:T(8,128)(2,1)}), bf16[128,1,30,128]{3,2,1,0:T(8,128)(2,1)S(1)}, u32[]{:S(2)}, u32[]{:S(2)}) async-start(bf16[128,1,30,128]{3,2,1,0:T(8,128)(2,1)} %constant_dynamic-update-slice_fusion.128), calls=%async_computation.3 | async-start | bytes 2097152 | tf_op jit(solution)/shard_map/all_to_all | solution.py:111
  504.3 10.2 %all-to-all-done.3 = bf16[128,1,30,128]{3,2,1,0:T(8,128)(2,1)S(1)} async-done(((bf16[128,1,30,128]{3,2,1,0:T(8,128)(2,1)}), bf16[128,1,30,128]{3,2,1,0:T(8,128)(2,1)S(1)}, u32[]{:S(2)}, u32[]{:S(2)}) %all-to-all-start.3) | async-done | bytes 983072 | tf_op jit(solution)/shard_map/all_to_all | solution.py:111
  514.4 5.0 all-to-all-start.1
  528.3 3.3 reshape.837
  533.9 3.5 pad_slice_fusion
  539.1 10.7 %all-to-all-start.4 = ((f32[128,1,2688]{2,1,0:T(1,128)}), f32[128,1,2688]{2,1,0:T(1,128)}, u32[]{:S(2)}, u32[]{:S(2)}) async-start(f32[128,1,2688]{2,1,0:T(1,128)} %bitcast.1443), calls=%async_computation.4 | async-start | bytes 2752512 | tf_op jit(solution)/shard_map/all_to_all | solution.py:125
  549.9 3.6 convolution_add_fusion.7
  563.0 9.0 %all-to-all-done.4 = f32[128,1,2688]{2,1,0:T(1,128)} async-done(((f32[128,1,2688]{2,1,0:T(1,128)}), f32[128,1,2688]{2,1,0:T(1,128)}, u32[]{:S(2)}, u32[]{:S(2)}) %all-to-all-start.4) | async-done | bytes 1376288 | tf_op jit(solution)/shard_map/all_to_all | solution.py:125
  575.9 4.3 all-to-all-start.5
  586.0 16.7 %all-to-all-done.5 = f32[128,1,2688]{2,1,0:T(1,128)S(1)} async-done(((f32[128,1,2688]{2,1,0:T(1,128)}), f32[128,1,2688]{2,1,0:T(1,128)S(1)}, u32[]{:S(2)}, u32[]{:S(2)}) %all-to-all-start.5) | async-done | bytes 1376288 | tf_op jit(solution)/shard_map/all_to_all | solution.py:130
  (492 shorter events, 295.0 us)
Async XLA Ops:
  0.6 7.3 %copy-start.42 = (bf16[9,128,128]{2,1,0:T(8,128)(2,1)S(1)}, bf16[9,128,128]{2,1,0:T(8,128)(2,1)}, u32[]{:S(2)}) copy-start(bf16[9,128,128]{2,1,0:T(8,128)(2,1)} %param.8) | copy-start | bytes 884740
  12.4 59.6 %copy-start = (f32[3840,128]{1,0:T(8,128)}, f32[3840,128]{1,0:T(8,128)S(1)}, u32[]{:S(2)}) copy-start(f32[3840,128]{1,0:T(8,128)S(1)} %convolution_add_fusion.24) | copy-start | bytes 5898244
  51.8 13.1 %copy-start.57 = (s32[2]{0:T(128)S(1)}, s32[2]{0:T(128)}, u32[]{:S(2)}) copy-start(s32[2]{0:T(128)} %param.12) | copy-start | bytes 28
  53.1 54.7 %all-to-all-start = ((bf16[128,2,1920]{2,1,0:T(2,128)(2,1)}), bf16[128,2,1920]{2,1,0:T(2,128)(2,1)S(1)}, u32[]{:S(2)}, u32[]{:S(2)}) async-start(bf16[128,2,1920]{2,1,0:T(2,128)(2,1)} %reshape.863), calls=%async_computation | async-start | bytes 1966080 | tf_op jit(solution)/shard_map/all_to_all | solution.py:106
  82.6 25.1 %copy-start.58 = (s32[8]{0:T(128)S(1)}, s32[8]{0:T(128)}, u32[]{:S(2)}) copy-start(s32[8]{0:T(128)} %param.11) | copy-start | bytes 100
  108.7 108.1 %all-to-all-start.2 = ((bf16[128,2,1920]{2,1,0:T(2,128)(2,1)}), bf16[128,2,1920]{2,1,0:T(2,128)(2,1)}, u32[]{:S(2)}, u32[]{:S(2)}) async-start(bf16[128,2,1920]{2,1,0:T(2,128)(2,1)} %reshape.865), calls=%async_computation.2 | async-start | bytes 1966080 | tf_op jit(solution)/shard_map/all_to_all | solution.py:106
  123.7 47.5 %copy-start.3 = (bf16[3840,1,128]{2,1,0:T(2,128)(2,1)}, bf16[3840,1,128]{2,1,0:T(2,128)(2,1)S(1)}, u32[]{:S(2)}) copy-start(bf16[3840,1,128]{2,1,0:T(2,128)(2,1)S(1)} %reshape.864) | copy-start | bytes 2949124
  168.3 1.7 copy-start.31
  176.4 1.3 copy-start.23
  182.7 4.1 copy-start.2
  186.8 4.9 copy-start.12
  191.7 4.2 copy-start.10
  195.9 4.2 copy-start.15
  240.1 2.6 copy-start.55
  277.0 1.7 copy-start.30
  278.7 1.6 copy-start.17
  278.7 2.1 copy-start.40
  280.9 1.7 copy-start.27
  282.6 1.6 copy-start.39
  282.6 1.8 copy-start.46
  293.2 3.0 copy-start.14
  302.8 3.0 copy-start.49
  309.9 3.0 copy-start.19
  313.0 74.3 %copy-start.13 = (bf16[128,30,128]{0,2,1:T(8,128)(2,1)S(1)}, bf16[128,30,128]{0,2,1:T(8,128)(2,1)}, u32[]{:S(2)}) copy-start(bf16[128,30,128]{0,2,1:T(8,128)(2,1)} %get-tuple-element.24) | copy-start | bytes 2949124
  313.0 74.3 %copy-start.51 = (f32[5,128,128]{2,1,0:T(8,128)S(1)}, f32[5,128,128]{2,1,0:T(8,128)}, u32[]{:S(2)}) copy-start(f32[5,128,128]{2,1,0:T(8,128)} %fusion.13) | copy-start | bytes 983044
  313.4 74.3 %copy-start.18 = (bf16[8,16,30,128]{3,2,1,0:T(8,128)(2,1)}, bf16[8,16,30,128]{3,2,1,0:T(8,128)(2,1)S(1)}, u32[]{:S(2)}) copy-start(bf16[8,16,30,128]{3,2,1,0:T(8,128)(2,1)S(1)} %add_convert_fusion) | copy-start | bytes 2949124
  318.2 69.5 %copy-start.43 = (bf16[128,30,128]{2,1,0:T(8,128)(2,1)S(1)}, bf16[128,30,128]{2,1,0:T(8,128)(2,1)}, u32[]{:S(2)}) copy-start(bf16[128,30,128]{2,1,0:T(8,128)(2,1)} %convert_element_type.204) | copy-start | bytes 2949124
  318.2 69.5 %copy-start.59 = (bf16[8,16,30,128]{3,2,1,0:T(8,128)(2,1)S(1)}, bf16[8,16,30,128]{3,2,1,0:T(8,128)(2,1)}, u32[]{:S(2)}) copy-start(bf16[8,16,30,128]{3,2,1,0:T(8,128)(2,1)} %get-tuple-element.5) | copy-start | bytes 2949124
  388.6 1.3 copy-start.53
  389.0 1.6 copy-start.4
  389.0 1.9 copy-start.44
  389.9 1.5 copy-start.52
  389.9 1.5 copy-start.7
  393.0 3.2 copy-start.34
  396.2 1.6 copy-start.33
  466.5 31.0 %copy-start.56 = (f32[1,128,128]{2,1,0:T(8,128)S(1)}, f32[1,128,128]{2,1,0:T(8,128)}, u32[]{:S(2)}) copy-start(f32[1,128,128]{2,1,0:T(8,128)} %convolution_bitcast_fusion.1) | copy-start | bytes 196612
  485.7 28.7 %all-to-all-start.3 = ((bf16[128,1,30,128]{3,2,1,0:T(8,128)(2,1)}), bf16[128,1,30,128]{3,2,1,0:T(8,128)(2,1)S(1)}, u32[]{:S(2)}, u32[]{:S(2)}) async-start(bf16[128,1,30,128]{3,2,1,0:T(8,128)(2,1)} %constant_dynamic-update-slice_fusion.128), calls=%async_computation.3 | async-start | bytes 2097152 | tf_op jit(solution)/shard_map/all_to_all | solution.py:111
  495.5 23.9 %copy-start.16 = (f32[128,1,30,128]{3,2,0,1:T(8,128)S(1)}, f32[128,1,30,128]{3,2,0,1:T(8,128)}, u32[]{:S(2)}) copy-start(f32[128,1,30,128]{3,2,0,1:T(8,128)} %reshape.822) | copy-start | bytes 5898244
  514.4 24.7 %all-to-all-start.1 = ((bf16[128,1,30,128]{3,2,1,0:T(8,128)(2,1)}), bf16[128,1,30,128]{3,2,1,0:T(8,128)(2,1)}, u32[]{:S(2)}, u32[]{:S(2)}) async-start(bf16[128,1,30,128]{3,2,1,0:T(8,128)(2,1)} %constant_dynamic-update-slice_fusion), calls=%async_computation.1 | async-start | bytes 2097152 | tf_op jit(solution)/shard_map/all_to_all | solution.py:111
  521.2 1.5 copy-start.6
  528.3 3.3 copy-start.1
  539.1 32.8 %all-to-all-start.4 = ((f32[128,1,2688]{2,1,0:T(1,128)}), f32[128,1,2688]{2,1,0:T(1,128)}, u32[]{:S(2)}, u32[]{:S(2)}) async-start(f32[128,1,2688]{2,1,0:T(1,128)} %bitcast.1443), calls=%async_computation.4 | async-start | bytes 2752512 | tf_op jit(solution)/shard_map/all_to_all | solution.py:125
  555.0 2.2 copy-start.26
  557.2 2.1 copy-start.25
  559.3 1.5 copy-start.41
  574.1 6.1 %copy-start.22 = (bf16[1,32,120,128]{3,2,1,0:T(8,128)(2,1)S(1)}, bf16[1,32,120,128]{3,2,1,0:T(8,128)(2,1)}, u32[]{:S(2)}) copy-start(bf16[1,32,120,128]{3,2,1,0:T(8,128)(2,1)} %get-tuple-element.11) | copy-start | bytes 2949124
  575.9 26.8 %all-to-all-start.5 = ((f32[128,1,2688]{2,1,0:T(1,128)}), f32[128,1,2688]{2,1,0:T(1,128)S(1)}, u32[]{:S(2)}, u32[]{:S(2)}) async-start(f32[128,1,2688]{2,1,0:T(1,128)} %broadcast_in_dim.5), calls=%async_computation.5 | async-start | bytes 2752512 | tf_op jit(solution)/shard_map/all_to_all | solution.py:130
  580.2 2.1 copy-start.21
  (18 other events, 21.5 us)
